TPU v7x, 32 devices: a whole 2x2x4 slice. The times are simulated.
32 devices in a mesh: groups: 1, row: 32 (over z, y, x, core).
Axes of the slice: x: 2, y: 2, z: 4, core: 2. Of those that a mesh axis runs over, the one named last changes fastest.
Arguments:
- latents: bfloat16 [2048, 1024], P(('groups', 'row')), may hold values from -6 to 6
- expert_ids: int32 [2048, 22], P(('groups', 'row')), may hold values from 0 to 63, all different within a row; in each aligned block of 64 rows (0 to 63, 64 to 127, ...) at most 33 rows name the same one
- gates: float32 [2048, 22], P(('groups', 'row')), may hold values from 0.02 to 0.2
- w_up: bfloat16 [64, 1024, 1344], P('row'), may hold values from -0.1875 to 0.1875
- w_down: bfloat16 [64, 1344, 1024], P('row'), may hold values from -0.15625 to 0.15625
Outputs:
- combined: bfloat16 [2048, 1024], P(('groups', 'row'))
Inputs may be any that keep to these rules, and one draw needn't show every extreme that they name: `expert_ids`: in each aligned block of 64 rows, each expert is named by at most 33 rows, a bound that some block reaches; a row names 22 different experts.
All inputs are finite; a program needn't handle non-finite values.
Results may differ from a plain program's by a relative error of at most 0.0058.
Values may be sent and summed in bfloat16 or wider, within the bound.
A program may use at most 64 MiB of HBM per device.

v0:
```python
import jax
import jax.numpy as jnp
from jax import lax
from jax.sharding import PartitionSpec as P


def slot_numbers(flat_ids, experts):
    labels = jnp.arange(experts, dtype=jnp.int32)
    onehot = (flat_ids[:, None] == labels[None, :]).astype(jnp.int32)
    before = jnp.cumsum(onehot, axis=0) - onehot
    return jnp.sum(before * onehot, axis=1)


def body(latents, expert_ids, gates, w_up, w_down):
    devices = lax.axis_size("row")
    local_experts = w_up.shape[0]
    experts = devices * local_experts
    tok_dev = expert_ids.shape[0]
    top_count = expert_ids.shape[1]
    feature_width = latents.shape[1]
    capacity = min(tok_dev, 3 * tok_dev * top_count // (2 * experts))
    flat_ids = expert_ids.reshape(-1)
    slot_rank = slot_numbers(flat_ids, experts)
    places = flat_ids * capacity + slot_rank
    padded = jnp.concatenate([latents, jnp.zeros((1, feature_width), latents.dtype)], axis=0)
    owners = jnp.arange(tok_dev * top_count, dtype=jnp.int32) // top_count
    lookup = jnp.full((experts * capacity,), tok_dev, jnp.int32).at[places].set(owners)
    buffer = padded[lookup].reshape(devices, local_experts, capacity, feature_width)
    hidden = jnp.einsum(
        "nekl,elh->nekh",
        lax.all_to_all(buffer, "row", split_axis=0, concat_axis=0, tiled=True),
        w_up,
        preferred_element_type=jnp.float32,
    )
    active = jnp.square(jnp.maximum(hidden, 0.0)).astype(jnp.bfloat16)
    output = jnp.einsum(
        "nekh,ehl->nekl", active, w_down, preferred_element_type=jnp.float32
    ).astype(jnp.bfloat16)
    returned = lax.all_to_all(output, "row", split_axis=0, concat_axis=0, tiled=True)
    results = returned.reshape(experts * capacity, feature_width)[places].reshape(
        tok_dev, top_count, feature_width
    )
    combined = jnp.sum(gates[:, :, None] * results.astype(jnp.float32), axis=1)
    return combined.astype(jnp.bfloat16)


def solution(mesh):
    in_specs = (
        P(("groups", "row"), None),
        P(("groups", "row"), None),
        P(("groups", "row"), None),
        P("row", None, None),
        P("row", None, None),
    )
    out_specs = P(("groups", "row"), None)
    return jax.shard_map(body, mesh=mesh, in_specs=in_specs, out_specs=out_specs, check_vma=False)
```

profile of v0, /device:TPU:0, one launch (start us, length us, event | category | flops | bytes accessed | tf_op | source)
XLA Modules:
  0.0 326.0 jit_solution(11784149561039595795)
XLA Ops:
  0.0 0.8 copy.16
  0.8 0.1 eq.29
  0.9 0.1 eq.25
  1.1 0.7 broadcast_multiply_fusion
  1.8 18.1 %reduce-window.6 = s32[64,11,128]{2,1,0:T(8,128)S(1)} reduce-window(s32[64,11,128]{2,1,0:T(8,128)S(1)} %fusion.9, s32[]{:T(128)} %constant.13.clone.1), window={size=1x1x128 pad=0_0x0_0x127_0}, to_apply=%region_0.0 | reduce-window | flops 11444224 | bytes 720900 | tf_op jit(solution)/shard_map/reduce-window
  20.0 0.2 slice.12
  20.2 0.3 copy.18
  20.5 0.1 copy.19
  20.6 0.2 broadcast_add_fusion
  20.8 0.1 copy.15
  20.9 0.1 mul.30
  21.0 0.2 fusion.12
  21.2 7.6 %scatter_custom_fusion = s32[2112]{0:T(1024)S(1)} fusion(s32[1408]{0:T(1024)S(1)} %fusion.18, s32[1408]{0:T(1024)S(1)} %add_select_fusion, s32[]{:T(128)} %constant.11.clone.1), kind=kCustom, calls=%fused_computation.31 | custom fusion | bytes 8452 | tf_op jit(solution)/shard_map/scatter | solution.py:27
  28.9 0.9 concatenate.3
  29.8 8.0 %gather_fusion = bf16[2112,1024]{1,0:T(8,128)(2,1)} fusion(bf16[65,1024]{1,0:T(8,128)(2,1)S(1)} %concatenate.3, s32[3072]{0:T(1024)S(1)} %pad_clamp_fusion), kind=kCustom, calls=%fused_computation | custom fusion | bytes 8659200 | tf_op jit(solution)/shard_map/gather | solution.py:28
  37.8 7.3 %reshape.57 = bf16[32,2,33,1024]{3,2,1,0:T(8,128)(2,1)} reshape(bf16[2112,1024]{1,0:T(8,128)(2,1)} %gather_fusion) | data formatting | bytes 8650752 | tf_op jit(solution)/shard_map/reshape | solution.py:28
  45.1 9.1 %copy.20 = bf16[32,2,33,1024]{3,1,2,0:T(2,128)(2,1)} copy(bf16[32,2,33,1024]{3,2,1,0:T(8,128)(2,1)} %reshape.57) | data formatting | bytes 8650752 | tf_op jit(solution)/shard_map/reshape | solution.py:28
  54.2 0.0 slice-start
  54.2 105.4 %all_to_all.10 = bf16[32,2,33,1024]{3,1,2,0:T(2,128)(2,1)S(1)} all-to-all(bf16[32,2,33,1024]{3,1,2,0:T(2,128)(2,1)} %copy.20), channel_id=1, replica_groups=mesh['groups'=1,'row'=32] {'row'}, dimensions={0} | all-to-all | bytes 8650752 | tf_op jit(solution)/shard_map/all_to_all | solution.py:31
  159.6 0.0 slice-start.1
  159.6 13.2 %multiply_convert_fusion = bf16[2,32,33,1344]{3,2,1,0:T(8,128)(2,1)} fusion(bf16[2,1024,1344]{1,2,0:T(8,128)(2,1)} %param.8, bf16[32,2,33,1024]{3,1,2,0:T(2,128)(2,1)S(1)} %all_to_all.10), kind=kOutput, calls=%fused_computation.3 | convolution fusion | flops 5821820928 | bytes 15507456 | tf_op jit(solution)/shard_map/nekl,elh->nekh/dot_general | solution.py:29
  172.8 0.0 slice-done
  172.8 0.0 slice-done.1
  172.8 12.1 %convert_bitcast_fusion = bf16[32,2,33,1024]{3,2,0,1:T(8,128)(2,1)} fusion(bf16[2,1344,1024]{2,1,0:T(8,128)(2,1)S(1)} %bitcast.42, bf16[2,32,33,1344]{3,2,1,0:T(8,128)(2,1)} %multiply_convert_fusion), kind=kOutput, calls=%fused_computation.10 | convolution fusion | flops 5815468032 | bytes 15507456 | tf_op jit(solution)/shard_map/nekh,ehl->nekl/dot_general | solution.py:36
  184.9 9.0 %copy.22 = bf16[32,2,33,1024]{3,1,2,0:T(2,128)(2,1)} copy(bf16[32,2,33,1024]{3,2,0,1:T(8,128)(2,1)} %convert_bitcast_fusion) | data formatting | bytes 8650752 | tf_op jit(solution)/shard_map/convert_element_type | solution.py:38
  193.9 0.0 copy-start
  193.9 3.9 %all-to-all-start.1 = ((bf16[32,2,33,1024]{3,1,2,0:T(2,128)(2,1)}), bf16[32,2,33,1024]{3,1,2,0:T(2,128)(2,1)}, u32[]{:S(2)}, u32[]{:S(2)}) async-start(bf16[32,2,33,1024]{3,1,2,0:T(2,128)(2,1)} %copy.22), calls=%async_computation.1 | async-start | bytes 8650752 | tf_op jit(solution)/shard_map/all_to_all | solution.py:39
  197.8 0.0 copy-done
  197.8 0.1 copy.14
  197.9 96.7 %all-to-all-done.1 = bf16[32,2,33,1024]{3,1,2,0:T(2,128)(2,1)} async-done(((bf16[32,2,33,1024]{3,1,2,0:T(2,128)(2,1)}), bf16[32,2,33,1024]{3,1,2,0:T(2,128)(2,1)}, u32[]{:S(2)}, u32[]{:S(2)}) %all-to-all-start.1) | async-done | bytes 4325408 | tf_op jit(solution)/shard_map/all_to_all | solution.py:39
  294.6 6.2 %copy.23 = bf16[32,2,33,1024]{3,2,1,0:T(8,128)(2,1)} copy(bf16[32,2,33,1024]{3,1,2,0:T(2,128)(2,1)} %all-to-all-done.1) | data formatting | bytes 8650752 | tf_op jit(solution)/shard_map/all_to_all | solution.py:39
  300.9 7.4 %reshape.58 = bf16[2112,1024]{1,0:T(8,128)(2,1)} reshape(bf16[32,2,33,1024]{3,2,1,0:T(8,128)(2,1)} %copy.23) | data formatting | bytes 8650752 | tf_op jit(solution)/shard_map/reshape | solution.py:40
  308.3 10.0 %gather_fusion.1 = bf16[1408,1024]{1,0:T(8,128)(2,1)S(1)} fusion(bf16[2112,1024]{1,0:T(8,128)(2,1)} %reshape.58, s32[2048]{0:T(1024)S(1)} %pad_clamp_fusion.1), kind=kCustom, calls=%fused_computation.1 | custom fusion | bytes 5772800 | tf_op jit(solution)/shard_map/gather | solution.py:40
  318.3 3.2 reshape.59
  321.5 4.5 %multiply_reduce_fusion = bf16[64,1024]{1,0:T(8,128)(2,1)} fusion(f32[64,22,1024]{2,1,0:T(8,128)} %reshape.59, f32[64,22]{1,0:T(8,128)S(1)} %copy.14), kind=kLoop, calls=%fused_computation.6 | loop fusion | flops 2818048 | bytes 5903872 | tf_op jit(solution)/shard_map/reduce_sum | solution.py:43
  (8 shorter events, 0.1 us)
Async XLA Ops:
  54.2 118.6 %slice-start = ((s8[5505024]{0:T(1024)(128)(4,1)}), s8[4194304]{0:T(1024)(128)(4,1)S(1)}, s32[]{:S(2)}) async-start(s8[5505024]{0:T(1024)(128)(4,1)} %bitcast.41), calls=%async_computation.2 | async-start | bytes 8388608
  159.6 13.2 %slice-start.1 = ((s8[5505024]{0:T(1024)(128)(4,1)}), s8[1310720]{0:T(1024)(128)(4,1)S(1)}, s32[]{:S(2)}) async-start(s8[5505024]{0:T(1024)(128)(4,1)} %bitcast.41), calls=%async_computation.3 | async-start | bytes 2621440
  193.9 3.9 %copy-start = (f32[64,22]{0,1:T(8,128)S(1)}, f32[64,22]{0,1:T(8,128)}, u32[]{:S(2)}) copy-start(f32[64,22]{0,1:T(8,128)} %param.7) | copy-start | bytes 16900
  193.9 100.8 %all-to-all-start.1 = ((bf16[32,2,33,1024]{3,1,2,0:T(2,128)(2,1)}), bf16[32,2,33,1024]{3,1,2,0:T(2,128)(2,1)}, u32[]{:S(2)}, u32[]{:S(2)}) async-start(bf16[32,2,33,1024]{3,1,2,0:T(2,128)(2,1)} %copy.22), calls=%async_computation.1 | async-start | bytes 8650752 | tf_op jit(solution)/shard_map/all_to_all | solution.py:39
where the time goes:
time: 327 us; the launch traced here: 326 us
  blocking collectives  105 us (32%)
  waiting for transfers between devices  96.7 us (30%)
  local copies, waits for them, and re-layouts  70.8 us (22%)
  matrix products  25.3 us (8%)
  other arithmetic  23.9 us (7%)
  starting transfers between devices  3.91 us (1%)
    all_to_all x1, blocking collectives, body(): lax.all_to_all(buffer, 'row', split_axis=0, concat_axis=0, tiled=True)  105 us
    all_to_all x1, waiting for transfers between devices, body(): lax.all_to_all(output, 'row', split_axis=0, concat_axis=0, tiled=True)  96.7 us
    another operation x3, other arithmetic  18.4 us
    reshape x2, local copies, waits for them, and re-layouts, body(): padded[lookup].reshape(devices, local_experts, capacity, feature_width)  16.4 us
    dot_general x1, matrix products, body(): jnp.einsum('nekl,elh->nekh', lax.all_to_all(buffer, 'row', split_axis=0,...  13.2 us
    dot_general x1, matrix products, body(): jnp.einsum('nekh,ehl->nekl', active, w_down, preferred_element_type=jnp.f...  12.1 us
    gather x1, local copies, waits for them, and re-layouts, body(): returned.reshape(experts * capacity, feature_width)[places]  10 us
    convert_element_type x1, local copies, waits for them, and re-layouts, body(): output = jnp.einsum('nekh,ehl->nekl', active, w_down, preferred_element_t...  9.01 us
  transfers between devices with their start and end apart: 1, of which 1 were waited for; matrix products, arithmetic and copies ran while one was open for 0% of the time, Pallas kernels for 0%

commit v1 on v0

v1 whole, which is shorter than its diff:
```python
import functools
import jax
import jax.numpy as jnp
from jax import lax
from jax.experimental import pallas as pl
from jax.experimental.pallas import tpu as pltpu
from jax.sharding import PartitionSpec as P

CORES = 2


def kernel(Z, Q, experts, xin, wu_hbm, wd_hbm, out, X, wu, wd, PP, RP, R, DH, XY, S, ZR, F, sel, sa, ra, sr, rr, wsem):
    T, W = xin.shape
    local_experts, L, H = wu.shape
    G = W - L
    half = T // 2
    layer = CORES * Q
    me = lax.axis_index("row")
    c = lax.rem(me, CORES)
    q = lax.rem(me // CORES, Q)
    z = me // layer
    inner = lax.rem(me, layer)
    partner = me + 1 - 2 * c
    if Q > 1:
        x = lax.rem(q, 2)
        y = q // 2
        xn, yn = me + CORES * (1 - 2 * x), me + 2 * CORES * (1 - 2 * y)
        qx, qy, qd = q + 1 - 2 * x, q + 2 * (1 - 2 * y), 3 - q

    def remote(src, dst, ssem, rsem, dev):
        return pltpu.make_async_remote_copy(
            src_ref=src, dst_ref=dst, send_sem=ssem, recv_sem=rsem,
            device_id={"row": dev}, device_id_type=pl.DeviceIdType.MESH,
        )

    weights = [
        pltpu.make_async_copy(wu_hbm, wu, wsem.at[0]),
        pltpu.make_async_copy(wd_hbm, wd, wsem.at[1]),
    ]
    local = pltpu.make_async_copy(xin, X.at[0, c, q], wsem.at[2])
    local.start()
    for w in weights:
        w.start()

    barrier = pltpu.get_barrier_semaphore()
    near = [partner] + ([xn, yn] if Q > 1 else [])
    for dev in near:
        pl.semaphore_signal(barrier, inc=1, device_id={"row": dev}, device_id_type=pl.DeviceIdType.MESH)

    def below(k):
        return lax.rem(z - k + Z, Z) * layer + inner

    def above(k):
        return lax.rem(z + k, Z) * layer + inner

    def greet(k, carry):
        pl.semaphore_signal(barrier, inc=1, device_id={"row": below(k)}, device_id_type=pl.DeviceIdType.MESH)
        return carry

    lax.fori_loop(1, Z, greet, 0)
    pl.semaphore_wait(barrier, len(near) + Z - 1)

    def zcopy(k):
        return remote(xin, X.at[k, c, q], sa.at[k, 0], ra.at[k, 0], below(k))

    def xcopy(k):
        return remote(X.at[k, c, q], X.at[k, c, q], sa.at[k, 1], ra.at[k, 1], xn)

    def ycopy(k):
        return remote(X.at[k, c, q], X.at[k, c, q], sa.at[k, 2], ra.at[k, 2], yn)

    def top(k, slot):
        ref = X.at[k, c, slot, pl.ds(0, half)]
        return remote(ref, ref, sa.at[k, 3], ra.at[k, 3], yn)

    def bottom(k, slot):
        ref = X.at[k, c, slot, pl.ds(half, half)]
        return remote(ref, ref, sa.at[k, 4], ra.at[k, 4], xn)

    def across(k, slot, i, plane):
        ref = X.at[k, plane, slot]
        return remote(ref, ref, sa.at[k, 5 + i], ra.at[k, 5 + i], partner)

    def arrived(k, ref, i):
        remote(ref, ref, sa.at[k, i], ra.at[k, i], partner).wait_recv()

    def ag_send(k):
        if Q > 1:
            xcopy(k).start()
            ycopy(k).start()
        across(k, q, 0, c).start()

    def ag_relay(k):
        if Q > 1:
            arrived(k, X.at[k, c, qx], 1)
            top(k, qx).start()
            arrived(k, X.at[k, c, qy], 2)
            bottom(k, qy).start()
            across(k, qx, 1, c).start()
            across(k, qy, 2, c).start()

    def ag_last(k):
        if Q > 1:
            arrived(k, X.at[k, c, qd, pl.ds(0, half)], 3)
            arrived(k, X.at[k, c, qd, pl.ds(half, half)], 4)
            across(k, qd, 3, c).start()

    def ag_other(k):
        arrived(k, X.at[k, 1 - c, q], 5)
        if Q > 1:
            arrived(k, X.at[k, 1 - c, qx], 6)
            arrived(k, X.at[k, 1 - c, qy], 7)
            arrived(k, X.at[k, 1 - c, qd], 8)

    def compute(k, plane):
        rows = X[k, plane, :, :, pl.ds(0, L)].reshape(Q * T, L)
        codes = X[k, plane, :, :, pl.ds(L, G)].reshape(Q * T, G)
        weight = jnp.dot(codes, sel[...], preferred_element_type=jnp.float32)
        total = None
        for e in range(local_experts):
            hidden = jnp.dot(rows, wu[e], preferred_element_type=jnp.float32)
            active = jnp.square(jnp.maximum(hidden, 0.0)).astype(jnp.bfloat16)
            part = jnp.dot(active, wd[e], preferred_element_type=jnp.float32)
            part = part * jnp.tile(weight[:, e * 128 : (e + 1) * 128], (1, L // 128))
            total = part if total is None else total + part
        return total

    def swap(k):
        return remote(PP.at[k], RP.at[k], sr.at[k, 0], rr.at[k, 0], partner)

    def dtop(k):
        return remote(R.at[k, qd, pl.ds(0, half)], DH.at[k, 0], sr.at[k, 1], rr.at[k, 1], yn)

    def dbottom(k):
        return remote(R.at[k, qd, pl.ds(half, half)], DH.at[k, 1], sr.at[k, 2], rr.at[k, 2], xn)

    def xsum(k):
        return remote(R.at[k, qx], XY.at[k, 0], sr.at[k, 3], rr.at[k, 3], xn)

    def ysum(k):
        return remote(R.at[k, qy], XY.at[k, 1], sr.at[k, 4], rr.at[k, 4], yn)

    def zsum(k):
        return remote(S.at[k], ZR.at[k], sr.at[k, 5], rr.at[k, 5], above(k))

    def rs_near(k):
        if Q > 1:
            dtop(k).wait_recv()
            R[k, qx, pl.ds(0, half)] = (
                R[k, qx, pl.ds(0, half)].astype(jnp.float32) + DH[k, 0].astype(jnp.float32)
            ).astype(jnp.bfloat16)
            xsum(k).start()
            dbottom(k).wait_recv()
            R[k, qy, pl.ds(half, half)] = (
                R[k, qy, pl.ds(half, half)].astype(jnp.float32) + DH[k, 1].astype(jnp.float32)
            ).astype(jnp.bfloat16)
            ysum(k).start()

    def rs_far(k):
        value = R[k, q].astype(jnp.float32)
        if Q > 1:
            xsum(k).wait_recv()
            value = value + XY[k, 0].astype(jnp.float32)
            ysum(k).wait_recv()
            value = value + XY[k, 1].astype(jnp.float32)

        @pl.when(k == 0)
        def _():
            F[...] = value

        @pl.when(k > 0)
        def _():
            S[k] = value.astype(jnp.bfloat16)
            zsum(k).start()

    local.wait()
    ag_send(0)

    def send_down(k, carry):
        zcopy(k).start()
        return carry

    lax.fori_loop(1, Z, send_down, 0)
    entry = lax.rem(lax.broadcasted_iota(jnp.int32, sel.shape, 0), experts)
    lane = lax.broadcasted_iota(jnp.int32, sel.shape, 1) // 128
    used = lax.broadcasted_iota(jnp.int32, sel.shape, 0) < 2 * experts
    sel[...] = jnp.where((entry == me * local_experts + lane) & used, 1.0, 0.0).astype(jnp.bfloat16)
    ag_relay(0)
    ag_last(0)
    for w in weights:
        w.wait()

    def step(k, carry):
        ag_other(k)

        @pl.when(k + 1 < Z)
        def _():
            arrived(k + 1, X.at[k + 1, c, q], 0)
            ag_send(k + 1)

        PP[k] = compute(k, 1 - c).astype(jnp.bfloat16)
        swap(k).start()

        @pl.when(k > 0)
        def _():
            rs_near(k - 1)

        @pl.when(k + 1 < Z)
        def _():
            ag_relay(k + 1)

        mine = compute(k, c)
        swap(k).wait_recv()
        R[k] = (mine + RP[k].astype(jnp.float32)).astype(jnp.bfloat16).reshape(Q, T, L)
        if Q > 1:
            dtop(k).start()
            dbottom(k).start()

        @pl.when(k + 1 < Z)
        def _():
            ag_last(k + 1)

        @pl.when(k > 0)
        def _():
            rs_far(k - 1)

        return carry

    lax.fori_loop(0, Z, step, 0)
    rs_near(Z - 1)
    rs_far(Z - 1)

    def collect(k, carry):
        zsum(k).wait_recv()
        F[...] += ZR[k].astype(jnp.float32)
        return carry

    lax.fori_loop(1, Z, collect, 0)
    out[...] = F[...].astype(out.dtype)

    def drain(k, carry):
        across(k, q, 0, c).wait_send()
        swap(k).wait_send()
        if Q > 1:
            xcopy(k).wait_send()
            ycopy(k).wait_send()
            top(k, qx).wait_send()
            bottom(k, qy).wait_send()
            across(k, qx, 1, c).wait_send()
            across(k, qy, 2, c).wait_send()
            across(k, qd, 3, c).wait_send()
            dtop(k).wait_send()
            dbottom(k).wait_send()
            xsum(k).wait_send()
            ysum(k).wait_send()

        @pl.when(k > 0)
        def _():
            zcopy(k).wait_send()
            zsum(k).wait_send()

        return carry

    lax.fori_loop(0, Z, drain, 0)


def body(groups, latents, expert_ids, gates, w_up, w_down):
    n = lax.axis_size("row")
    T, L = latents.shape
    local_experts, unused, H = w_up.shape
    experts = n * local_experts
    Q = 4 if groups == 1 and n % (4 * CORES) == 0 else 1
    Z = n // (CORES * Q)
    labels = jnp.arange(experts, dtype=jnp.int32)
    dense = jnp.sum(
        jnp.where(expert_ids[:, :, None] == labels[None, None, :], gates[:, :, None], 0.0), axis=1
    )
    coarse = lax.reduce_precision(dense, 8, 7)
    G = -(-2 * experts // 128) * 128
    pad = jnp.zeros((T, G - 2 * experts), jnp.bfloat16)
    rows = jnp.concatenate(
        [latents, coarse.astype(jnp.bfloat16), (dense - coarse).astype(jnp.bfloat16), pad], axis=1
    )
    bf16 = jnp.bfloat16
    return pl.pallas_call(
        functools.partial(kernel, Z, Q, experts),
        out_shape=jax.ShapeDtypeStruct((T, L), bf16),
        in_specs=[
            pl.BlockSpec(memory_space=pltpu.VMEM),
            pl.BlockSpec(memory_space=pl.ANY),
            pl.BlockSpec(memory_space=pl.ANY),
        ],
        out_specs=pl.BlockSpec(memory_space=pltpu.VMEM),
        scratch_shapes=[
            pltpu.VMEM((Z, CORES, Q, T, L + G), bf16),
            pltpu.VMEM(w_up.shape, bf16),
            pltpu.VMEM(w_down.shape, bf16),
            pltpu.VMEM((Z, Q * T, L), bf16),
            pltpu.VMEM((Z, Q * T, L), bf16),
            pltpu.VMEM((Z, Q, T, L), bf16),
            pltpu.VMEM((Z if Q > 1 else 1, 2, T // 2, L), bf16),
            pltpu.VMEM((Z if Q > 1 else 1, 2, T, L), bf16),
            pltpu.VMEM((Z, T, L), bf16),
            pltpu.VMEM((Z, T, L), bf16),
            pltpu.VMEM((T, L), jnp.float32),
            pltpu.VMEM((G, local_experts * 128), bf16),
            pltpu.SemaphoreType.DMA((Z, 9)),
            pltpu.SemaphoreType.DMA((Z, 9)),
            pltpu.SemaphoreType.DMA((Z, 6)),
            pltpu.SemaphoreType.DMA((Z, 6)),
            pltpu.SemaphoreType.DMA((3,)),
        ],
        compiler_params=pltpu.CompilerParams(
            collective_id=0, has_side_effects=True, vmem_limit_bytes=64 * 1024 * 1024 - 65536
        ),
    )(rows, w_up, w_down)


def solution(mesh):
    in_specs = (
        P(("groups", "row"), None),
        P(("groups", "row"), None),
        P(("groups", "row"), None),
        P("row", None, None),
        P("row", None, None),
    )
    out_specs = P(("groups", "row"), None)
    return jax.shard_map(
        functools.partial(body, mesh.shape["groups"]),
        mesh=mesh, in_specs=in_specs, out_specs=out_specs, check_vma=False,
    )
```

time: 327 us -> 83.5 us (0.26)
  blocking collectives: 105 us -> 0 us
  waiting for transfers between devices: 96.7 us -> 0 us
  Pallas kernels: 0 us -> 70.4 us
  local copies, waits for them, and re-layouts: 70.8 us -> 11.5 us
  matrix products: 25.3 us -> 0 us
  other arithmetic: 23.9 us -> 1.17 us
  starting transfers between devices: 3.91 us -> 0 us
    all_to_all x1 -> x0, blocking collectives: 105 us -> none  [body(): lax.all_to_all(buffer, 'row', split_axis=0, concat_axis=0, tiled=True)]
    all_to_all x1 -> x0, waiting for transfers between devices: 96.7 us -> none  [body(): lax.all_to_all(output, 'row', split_axis=0, concat_axis=0, tiled=True)]
    pallas_call x0 -> x1, Pallas kernels: none -> 70.4 us  [body(): pl.pallas_call(functools.partial(kernel, Z, Q, experts), out_shape=jax.Sh...]
    dot_general x2 -> x0, matrix products: 25.3 us -> none  [the longest x1 13.2 us: body(): jnp.einsum('nekl,elh->nekh', lax.all_to_all(buffer, 'row', split_axis=0,...]
    reshape x3 -> x0, local copies, waits for them, and re-layouts: 23.8 us -> none  [the longest x2 16.4 us: body(): padded[lookup].reshape(devices, local_experts, capacity, feature_width)]
    another operation x3 -> x0, other arithmetic: 18.4 us -> none
    gather x2 -> x0, local copies, waits for them, and re-layouts: 18 us -> none  [the longest x1 10 us: body(): returned.reshape(experts * capacity, feature_width)[places]]
    convert_element_type x2 -> x0, local copies, waits for them, and re-layouts: 12.2 us -> none  [the longest x1 9.01 us: body(): output = jnp.einsum('nekh,ehl->nekl', active, w_down, preferred_element_t...]
  transfers between devices with their start and end apart: 1 -> 0, of which waited for: 1 -> 0; matrix products, arithmetic and copies ran while one was open for 0% -> 0% of each run, Pallas kernels for 0% -> 0%
where the time goes in v1:
time: 83.5 us; the launch traced here: 83.1 us
  Pallas kernels  70.4 us (84%)
  local copies, waits for them, and re-layouts  11.5 us (14%)
  other arithmetic  1.17 us (1%)
    pallas_call x1, Pallas kernels, body(): pl.pallas_call(functools.partial(kernel, Z, Q, experts), out_shape=jax.Sh...  70.4 us
    unnamed x2, local copies, waits for them, and re-layouts  9.87 us

profile of v1, /device:TPU:0, one launch (start us, length us, event | category | flops | bytes accessed | tf_op | source)
XLA Modules:
  0.0 83.1 jit_solution(15736070445624448644)
XLA Ops:
  0.0 1.2 %select_reduce_fusion = f32[64,64]{1,0:T(8,128)S(1)} fusion(f32[64,22]{0,1:T(8,128)} %param.7, s32[64,22]{0,1:T(8,128)} %param.6), kind=kLoop, calls=%fused_computation | loop fusion | flops 266240 | bytes 27648 | tf_op jit(solution)/shard_map/reduce_sum | solution.py:275
  1.2 1.7 %concatenate.3.xin = bf16[64,1152]{1,0:T(8,128)(2,1)} concatenate(bf16[64,1024]{1,0:T(8,128)(2,1)} %param.5, bf16[64,64]{1,0:T(8,128)(2,1)S(1)} %get-tuple-element.6, bf16[64,64]{1,0:T(8,128)(2,1)S(1)} %get-tuple-element.5), dimensions={1} | concatenate | bytes 294912 | tf_op jit(solution)/shard_map/concatenate | solution.py:281
  2.8 8.3 %copy.9.wu_hbm = bf16[2,1024,1344]{2,1,0:T(8,128)(2,1)} copy(bf16[2,1024,1344]{1,2,0:T(8,128)(2,1)} %param.8) | data formatting | bytes 11010048 | tf_op args[3]
  11.1 70.4 %shard_map.55 = bf16[64,1024]{1,0:T(8,128)(2,1)} custom-call(bf16[64,1152]{1,0:T(8,128)(2,1)} %concatenate.3.xin, bf16[2,1024,1344]{2,1,0:T(8,128)(2,1)} %copy.9.wu_hbm, bf16[2,1344,1024]{2,1,0:T(8,128)(2,1)} %wd_hbm.1), custom_call_target="tpu_custom_call" | custom-call | tf_op jit(solution)/shard_map/pallas_call | solution.py:285
  81.5 1.6 %copy.11 = bf16[64,1024]{1,0:T(8,128)(2,1)} copy(bf16[64,1024]{1,0:T(8,128)(2,1)} %shard_map.55) | data formatting | bytes 262144
  (1 shorter events, 0.0 us)

commit v2 on v1

--- a/solution.py
+++ b/solution.py
@@ -11,7 +11,7 @@
 
 def kernel(Z, Q, experts, xin, wu_hbm, wd_hbm, out, X, wu, wd, PP, RP, R, DH, XY, S, ZR, F, sel, sa, ra, sr, rr, wsem):
     T, W = xin.shape
-    local_experts, L, H = wu.shape
+    local_experts, H, L = wu.shape
     G = W - L
     half = T // 2
     layer = CORES * Q
@@ -118,7 +118,7 @@
         weight = jnp.dot(codes, sel[...], preferred_element_type=jnp.float32)
         total = None
         for e in range(local_experts):
-            hidden = jnp.dot(rows, wu[e], preferred_element_type=jnp.float32)
+            hidden = lax.dot_general(rows, wu[e], (((1,), (1,)), ((), ())), preferred_element_type=jnp.float32)
             active = jnp.square(jnp.maximum(hidden, 0.0)).astype(jnp.bfloat16)
             part = jnp.dot(active, wd[e], preferred_element_type=jnp.float32)
             part = part * jnp.tile(weight[:, e * 128 : (e + 1) * 128], (1, L // 128))
@@ -293,7 +293,7 @@
         out_specs=pl.BlockSpec(memory_space=pltpu.VMEM),
         scratch_shapes=[
             pltpu.VMEM((Z, CORES, Q, T, L + G), bf16),
-            pltpu.VMEM(w_up.shape, bf16),
+            pltpu.VMEM(w_down.shape, bf16),
             pltpu.VMEM(w_down.shape, bf16),
             pltpu.VMEM((Z, Q * T, L), bf16),
             pltpu.VMEM((Z, Q * T, L), bf16),
@@ -313,7 +313,7 @@
         compiler_params=pltpu.CompilerParams(
             collective_id=0, has_side_effects=True, vmem_limit_bytes=64 * 1024 * 1024 - 65536
         ),
-    )(rows, w_up, w_down)
+    )(rows, jnp.swapaxes(w_up,1,2), w_down)
 
 
 def solution(mesh):

time: 83.5 us -> 75.2 us (0.901)
  local copies, waits for them, and re-layouts: 11.5 us -> 3.21 us
    unnamed x2 -> x1, local copies, waits for them, and re-layouts: 9.87 us -> 1.57 us
where the time goes in v2:
time: 75.2 us; the launch traced here: 74.9 us
  Pallas kernels  70.5 us (94%)
  local copies, waits for them, and re-layouts  3.21 us (4%)
  other arithmetic  1.17 us (2%)
    pallas_call x1, Pallas kernels, body(): pl.pallas_call(functools.partial(kernel, Z, Q, experts), out_shape=jax.Sh...  70.5 us
    concatenate x1, local copies, waits for them, and re-layouts, body(): jnp.concatenate([latents, coarse.astype(jnp.bfloat16), (dense - coarse).a...  1.64 us
    unnamed x1, local copies, waits for them, and re-layouts  1.57 us

profile of v2, /device:TPU:0, one launch (start us, length us, event | category | flops | bytes accessed | tf_op | source)
XLA Modules:
  0.0 74.9 jit_solution(10896265112785416184)
XLA Ops:
  0.0 1.2 %select_reduce_fusion = f32[64,64]{1,0:T(8,128)S(1)} fusion(f32[64,22]{0,1:T(8,128)} %param.7, s32[64,22]{0,1:T(8,128)} %param.6), kind=kLoop, calls=%fused_computation | loop fusion | flops 266240 | bytes 27648 | tf_op jit(solution)/shard_map/reduce_sum | solution.py:275
  1.2 1.6 %concatenate.3.xin = bf16[64,1152]{1,0:T(8,128)(2,1)} concatenate(bf16[64,1024]{1,0:T(8,128)(2,1)} %param.5, bf16[64,64]{1,0:T(8,128)(2,1)S(1)} %get-tuple-element.6, bf16[64,64]{1,0:T(8,128)(2,1)S(1)} %get-tuple-element.5), dimensions={1} | concatenate | bytes 294912 | tf_op jit(solution)/shard_map/concatenate | solution.py:281
  2.8 70.5 %shard_map.55 = bf16[64,1024]{1,0:T(8,128)(2,1)} custom-call(bf16[64,1152]{1,0:T(8,128)(2,1)} %concatenate.3.xin, bf16[2,1344,1024]{2,1,0:T(8,128)(2,1)} %bitcast.1, bf16[2,1344,1024]{2,1,0:T(8,128)(2,1)} %wd_hbm.1), custom_call_target="tpu_custom_call" | custom-call | tf_op jit(solution)/shard_map/pallas_call | solution.py:285
  73.3 1.6 %copy.9 = bf16[64,1024]{1,0:T(8,128)(2,1)} copy(bf16[64,1024]{1,0:T(8,128)(2,1)} %shard_map.55) | data formatting | bytes 262144
  (1 shorter events, 0.0 us)

commit v3 on v2

--- a/solution.py
+++ b/solution.py
@@ -173,41 +173,49 @@
             S[k] = value.astype(jnp.bfloat16)
             zsum(k).start()
 
+    if Z > 1:
+        zcopy(1).start()
     local.wait()
     ag_send(0)
-
-    def send_down(k, carry):
-        zcopy(k).start()
-        return carry
-
-    lax.fori_loop(1, Z, send_down, 0)
     entry = lax.rem(lax.broadcasted_iota(jnp.int32, sel.shape, 0), experts)
     lane = lax.broadcasted_iota(jnp.int32, sel.shape, 1) // 128
     used = lax.broadcasted_iota(jnp.int32, sel.shape, 0) < 2 * experts
     sel[...] = jnp.where((entry == me * local_experts + lane) & used, 1.0, 0.0).astype(jnp.bfloat16)
     ag_relay(0)
+    if Z > 2:
+        zcopy(2).start()
+    if Z > 1:
+        arrived(1, X.at[1, c, q], 0)
+        ag_send(1)
     ag_last(0)
     for w in weights:
         w.wait()
 
     def step(k, carry):
         ag_other(k)
-
-        @pl.when(k + 1 < Z)
-        def _():
-            arrived(k + 1, X.at[k + 1, c, q], 0)
-            ag_send(k + 1)
-
         PP[k] = compute(k, 1 - c).astype(jnp.bfloat16)
         swap(k).start()
 
+        @pl.when(k + 1 < Z)
+        def _():
+            ag_relay(k + 1)
+
         @pl.when(k > 0)
         def _():
             rs_near(k - 1)
 
-        @pl.when(k + 1 < Z)
-        def _():
-            ag_relay(k + 1)
+        @pl.when(k + 2 < Z)
+        def _():
+            arrived(k + 2, X.at[k + 2, c, q], 0)
+            ag_send(k + 2)
+
+        @pl.when(k + 3 < Z)
+        def _():
+            zcopy(k + 3).start()
+
+        @pl.when(k > 1)
+        def _():
+            rs_far(k - 2)
 
         mine = compute(k, c)
         swap(k).wait_recv()
@@ -220,13 +228,11 @@
         def _():
             ag_last(k + 1)
 
-        @pl.when(k > 0)
-        def _():
-            rs_far(k - 1)
-
         return carry
 
     lax.fori_loop(0, Z, step, 0)
+    if Z > 1:
+        rs_far(Z - 2)
     rs_near(Z - 1)
     rs_far(Z - 1)
 

time: 75.2 us -> 68.5 us (0.911)
  Pallas kernels: 70.5 us -> 63.8 us
    pallas_call x1, Pallas kernels: 70.5 us -> 63.8 us  [body(): pl.pallas_call(functools.partial(kernel, Z, Q, experts), out_shape=jax.Sh...]
where the time goes in v3:
time: 68.5 us; the launch traced here: 68.2 us
  Pallas kernels  63.8 us (93%)
  local copies, waits for them, and re-layouts  3.21 us (5%)
  other arithmetic  1.17 us (2%)
    pallas_call x1, Pallas kernels, body(): pl.pallas_call(functools.partial(kernel, Z, Q, experts), out_shape=jax.Sh...  63.8 us
    concatenate x1, local copies, waits for them, and re-layouts, body(): jnp.concatenate([latents, coarse.astype(jnp.bfloat16), (dense - coarse).a...  1.64 us
    unnamed x1, local copies, waits for them, and re-layouts  1.57 us

profile of v3, /device:TPU:0, one launch (start us, length us, event | category | flops | bytes accessed | tf_op | source)
XLA Modules:
  0.0 68.2 jit_solution(445754846478240890)
XLA Ops:
  0.0 1.2 %select_reduce_fusion = f32[64,64]{1,0:T(8,128)S(1)} fusion(f32[64,22]{0,1:T(8,128)} %param.7, s32[64,22]{0,1:T(8,128)} %param.6), kind=kLoop, calls=%fused_computation | loop fusion | flops 266240 | bytes 27648 | tf_op jit(solution)/shard_map/reduce_sum | solution.py:281
  1.2 1.6 %concatenate.3.xin = bf16[64,1152]{1,0:T(8,128)(2,1)} concatenate(bf16[64,1024]{1,0:T(8,128)(2,1)} %param.5, bf16[64,64]{1,0:T(8,128)(2,1)S(1)} %get-tuple-element.6, bf16[64,64]{1,0:T(8,128)(2,1)S(1)} %get-tuple-element.5), dimensions={1} | concatenate | bytes 294912 | tf_op jit(solution)/shard_map/concatenate | solution.py:287
  2.8 63.8 %shard_map.55 = bf16[64,1024]{1,0:T(8,128)(2,1)} custom-call(bf16[64,1152]{1,0:T(8,128)(2,1)} %concatenate.3.xin, bf16[2,1344,1024]{2,1,0:T(8,128)(2,1)} %bitcast.1, bf16[2,1344,1024]{2,1,0:T(8,128)(2,1)} %wd_hbm.1), custom_call_target="tpu_custom_call" | custom-call | tf_op jit(solution)/shard_map/pallas_call | solution.py:291
  66.6 1.6 %copy.9 = bf16[64,1024]{1,0:T(8,128)(2,1)} copy(bf16[64,1024]{1,0:T(8,128)(2,1)} %shard_map.55) | data formatting | bytes 262144
  (1 shorter events, 0.0 us)

commit v4 on v3

--- a/solution.py
+++ b/solution.py
@@ -177,17 +177,19 @@
         zcopy(1).start()
     local.wait()
     ag_send(0)
+    if Z > 2:
+        zcopy(2).start()
     entry = lax.rem(lax.broadcasted_iota(jnp.int32, sel.shape, 0), experts)
     lane = lax.broadcasted_iota(jnp.int32, sel.shape, 1) // 128
     used = lax.broadcasted_iota(jnp.int32, sel.shape, 0) < 2 * experts
     sel[...] = jnp.where((entry == me * local_experts + lane) & used, 1.0, 0.0).astype(jnp.bfloat16)
     ag_relay(0)
-    if Z > 2:
-        zcopy(2).start()
+    if Z > 3:
+        zcopy(3).start()
+    ag_last(0)
     if Z > 1:
         arrived(1, X.at[1, c, q], 0)
         ag_send(1)
-    ag_last(0)
     for w in weights:
         w.wait()
 
@@ -209,9 +211,9 @@
             arrived(k + 2, X.at[k + 2, c, q], 0)
             ag_send(k + 2)
 
-        @pl.when(k + 3 < Z)
-        def _():
-            zcopy(k + 3).start()
+        @pl.when(k + 4 < Z)
+        def _():
+            zcopy(k + 4).start()
 
         @pl.when(k > 1)
         def _():

time: 68.5 us -> 71.8 us (1.048)
  Pallas kernels: 63.8 us -> 67.1 us
    pallas_call x1, Pallas kernels: 63.8 us -> 67.1 us  [body(): pl.pallas_call(functools.partial(kernel, Z, Q, experts), out_shape=jax.Sh...]
where the time goes in v4:
time: 71.8 us; the launch traced here: 71.5 us
  Pallas kernels  67.1 us (93%)
  local copies, waits for them, and re-layouts  3.21 us (4%)
  other arithmetic  1.17 us (2%)
    pallas_call x1, Pallas kernels, body(): pl.pallas_call(functools.partial(kernel, Z, Q, experts), out_shape=jax.Sh...  67.1 us
    concatenate x1, local copies, waits for them, and re-layouts, body(): jnp.concatenate([latents, coarse.astype(jnp.bfloat16), (dense - coarse).a...  1.64 us
    unnamed x1, local copies, waits for them, and re-layouts  1.57 us

profile of v4, /device:TPU:0, one launch (start us, length us, event | category | flops | bytes accessed | tf_op | source)
XLA Modules:
  0.0 71.5 jit_solution(17090510013735697858)
XLA Ops:
  0.0 1.2 %select_reduce_fusion = f32[64,64]{1,0:T(8,128)S(1)} fusion(f32[64,22]{0,1:T(8,128)} %param.7, s32[64,22]{0,1:T(8,128)} %param.6), kind=kLoop, calls=%fused_computation | loop fusion | flops 266240 | bytes 27648 | tf_op jit(solution)/shard_map/reduce_sum | solution.py:283
  1.2 1.6 %concatenate.3.xin = bf16[64,1152]{1,0:T(8,128)(2,1)} concatenate(bf16[64,1024]{1,0:T(8,128)(2,1)} %param.5, bf16[64,64]{1,0:T(8,128)(2,1)S(1)} %get-tuple-element.6, bf16[64,64]{1,0:T(8,128)(2,1)S(1)} %get-tuple-element.5), dimensions={1} | concatenate | bytes 294912 | tf_op jit(solution)/shard_map/concatenate | solution.py:289
  2.8 67.1 %shard_map.55 = bf16[64,1024]{1,0:T(8,128)(2,1)} custom-call(bf16[64,1152]{1,0:T(8,128)(2,1)} %concatenate.3.xin, bf16[2,1344,1024]{2,1,0:T(8,128)(2,1)} %bitcast.1, bf16[2,1344,1024]{2,1,0:T(8,128)(2,1)} %wd_hbm.1), custom_call_target="tpu_custom_call" | custom-call | tf_op jit(solution)/shard_map/pallas_call | solution.py:293
  69.9 1.6 %copy.9 = bf16[64,1024]{1,0:T(8,128)(2,1)} copy(bf16[64,1024]{1,0:T(8,128)(2,1)} %shard_map.55) | data formatting | bytes 262144
  (1 shorter events, 0.0 us)
